TPU v7x, 256 devices: a whole 4x4x8 slice. The times are simulated.
256 devices in a mesh: seq: 32 (over x, z), tensor: 8 (over y, core).
Axes of the slice: x: 4, y: 4, z: 8, core: 2. Of those that a mesh axis runs over, the one named last changes fastest.
Arguments:
- hidden_in: bfloat16 [8192, 4096], P(('seq', 'tensor')), may hold values from -30 to 30
- prev_amax: float32 [], replicated, may hold values from 5 to 9
- w_x: bfloat16 [4096, 8192], P('seq', 'tensor'), may hold values from -0.09375 to 0.09375
- w_bc: bfloat16 [4096, 8, 2, 128], P('seq', 'tensor'), may hold values from -0.046875 to 0.046875
- w_dt: bfloat16 [4096, 128], P('seq', 'tensor'), may hold values from -0.09375 to 0.09375
- conv_x: float32 [4, 8192], P(None, 'tensor'), may hold values from -4 to 4
- conv_bc: float32 [4, 8, 2, 128], P(None, 'tensor'), may hold values from -4 to 4
- conv_state_x: bfloat16 [3, 8192], P(None, 'tensor'), may hold values from -6 to 6
- conv_state_bc: bfloat16 [3, 8, 2, 128], P(None, 'tensor'), may hold values from -3 to 3
- dt_bias: float32 [128], P('tensor'), may hold values from -2 to 1
- decay_rate: float32 [128], P('tensor'), may hold values from 1.2207031e-05 to 0.12
- skip: float32 [128], P('tensor'), may hold values from 0.5 to 4
- init_state: float32 [128, 64, 128], P('tensor'), may hold values from -48 to 48
- norm_gain: float32 [8192], P('tensor'), may hold values from 0.1 to 1.9
- w_out: bfloat16 [8192, 4096], P('tensor', 'seq'), may hold values from -0.0625 to 0.0625
Outputs:
- layer_out: bfloat16 [8192, 4096], P(('seq', 'tensor'))
- abs_max: float32 [], replicated
All inputs are finite; a program needn't handle non-finite values.
Results may differ from a plain program's by a relative error of at most 0.019.
Values may be sent and summed in bfloat16 or wider, within the bound.
A program may use at most 64 MiB of HBM per device.

v0:
```python
import jax
import jax.numpy as jnp
from jax import lax
from jax.sharding import Mesh
from jax.sharding import PartitionSpec as P

HEADS = 128
HEAD_DIM = 64
STATE = 128
GROUPS = 8
KERNEL = 4
SPAN = 128
SEQ = ("seq_0", "seq_1")
SEQ_TENSOR = ("seq_0", "seq_1", "tensor")
epsilon = 1e-05
quant_range = 448.0


def in_order(parts, dim):
    dims = list(parts.shape[1:])
    dims[dim] *= parts.shape[0]
    return jnp.moveaxis(parts, 0, dim).reshape(dims)


def sent_to_all(shard, axis):
    count = lax.axis_size(axis)
    return lax.all_to_all(
        jnp.broadcast_to(shard[None], (count, *shard.shape)), axis, 0, 0, tiled=True
    )


def gather_directly(shard, axis, dim):
    return in_order(sent_to_all(shard, axis), dim)


def over_copies(shard, axis):
    everything = sent_to_all(shard, axis)
    return jnp.max(everything, axis=0)


def sent_together(arrays, axis, dim, along):
    ends, at = ([], 0)
    for a in arrays[:-1]:
        at += a.shape[along]
        ends.append(at)
    both = jnp.concatenate(arrays, axis=along)
    return tuple(jnp.split(lax.all_gather(both, axis, axis=dim, tiled=True), ends, axis=along))


def from_behind(value, axis, steps):
    count = lax.axis_size(axis)
    first, last = (max(0, -steps), min(count, count - steps))
    return lax.ppermute(value, axis, [(source, source + steps) for source in range(first, last)])


def neutral_like(shard, identity):
    return jax.tree.map(
        lambda a, e: jnp.broadcast_to(jnp.asarray(e, a.dtype), a.shape), shard, identity
    )


def prefix_by_axis(shard, axes, combine, identity):
    before = start = neutral_like(shard, identity)
    total = shard
    for axis in reversed(axes):
        count, here = (lax.axis_size(axis), lax.axis_index(axis))
        pieces = jax.tree.map(
            lambda part, kind: lax.all_gather(part.astype(kind), axis),
            total,
            (jnp.bfloat16, jnp.bfloat16),
        )
        inside, total = (start, start)
        for k in range(count):
            passed = k < here
            total = combine(
                total, jax.tree.map(lambda part, own: part[k].astype(own.dtype), pieces, shard)
            )
            inside = jax.tree.map(lambda new, old: jnp.where(passed, new, old), total, inside)
        before = combine(inside, before)
    return before


def taken_together(shard, axis):
    return sent_to_all(shard, axis).sum(axis=0)


def cut_along(shard, dim, count):
    before, after = (shard.shape[:dim], shard.shape[dim + 1 :])
    return jnp.moveaxis(shard.reshape(*before, count, -1, *after), dim, 0)


def sent_and_summed(shard, axis, dim):
    parts = cut_along(shard, dim, lax.axis_size(axis))
    arrived = lax.all_to_all(parts, axis, split_axis=0, concat_axis=0, tiled=True)
    return arrived.astype(jnp.float32).sum(axis=0)


def depthwise(before, projected, conv_taps, length):
    extended = jnp.concatenate([before, projected], axis=0)
    summed = conv_taps[0] * extended[0:length]
    for offset in range(1, KERNEL):
        summed = summed + conv_taps[offset] * extended[offset : offset + length]
    return jax.nn.silu(summed).astype(jnp.bfloat16)


def combine(earlier, later):
    return (earlier[0] * later[0], later[0][:, None, None] * earlier[1] + later[1])


def local(
    hidden_in,
    prev_amax,
    w_x,
    w_bc,
    w_dt,
    conv_x,
    conv_bc,
    conv_state_x,
    conv_state_bc,
    dt_bias,
    decay_rate,
    skip,
    init_state,
    norm_gain,
    w_out,
):
    margin = KERNEL - 1
    gathered = gather_directly(hidden_in, "tensor", 0)
    abs_max = over_copies(jnp.max(jnp.abs(gathered.astype(jnp.float32))), SEQ)
    in_scale = prev_amax / quant_range
    leading = lax.axis_index(SEQ) == 0
    row_count = gathered.shape[0]
    bc_width = w_bc.shape[1] * w_bc.shape[2] * w_bc.shape[3]
    bc_rows = jnp.reshape(w_bc, (w_bc.shape[0], bc_width))
    scaled = gathered.astype(jnp.float32) * (quant_range / prev_amax)
    quant = jnp.clip(scaled, -quant_range, quant_range).astype(jnp.bfloat16)
    pieces = sent_together((w_x, bc_rows, w_dt), SEQ, 0, 1)
    x_proj, bc_proj, dt_proj = tuple(
        (
            jnp.dot(quant, weight_piece, preferred_element_type=jnp.float32)
            for weight_piece in pieces
        )
    )
    x_whole = (x_proj * in_scale).astype(jnp.bfloat16)
    bc_whole = (bc_proj * in_scale).astype(jnp.bfloat16)
    dt_raw = dt_proj * in_scale
    state_bc = jnp.reshape(conv_state_bc, (margin, bc_width))
    received = from_behind((x_whole[row_count - margin :], bc_whole[row_count - margin :]), SEQ, 1)
    x_edge = jnp.where(leading, conv_state_x, received[0])
    bc_edge = jnp.where(leading, state_bc, received[1])
    x_act = depthwise(x_edge, x_whole, conv_x, row_count)
    bc_act = depthwise(bc_edge, bc_whole, jnp.reshape(conv_bc, (KERNEL, bc_width)), row_count)
    step_size = jax.nn.softplus(dt_raw + dt_bias)
    heads_here = step_size.shape[1]
    groups_here = w_bc.shape[1]
    per_group = HEADS // GROUPS
    blocks = row_count // SPAN
    x_blocks = x_act.reshape(blocks, SPAN, heads_here, HEAD_DIM)
    bc_blocks = bc_act.reshape(blocks, SPAN, groups_here, 2, STATE)
    in_map = bc_blocks[:, :, :, 0]
    out_map = bc_blocks[:, :, :, 1]
    step_blocks = step_size.reshape(blocks, SPAN, heads_here)
    cum_blocks = jnp.cumsum(-step_blocks * decay_rate, axis=1)
    index_row = jnp.arange(SPAN, dtype=jnp.int32)
    lower_mask = index_row[:, None] >= index_row[None, :]
    intersection = jnp.einsum(
        "ctgn,cugn->cgtu", out_map, in_map, preferred_element_type=jnp.float32
    )
    intersection = jnp.repeat(intersection, per_group, axis=1)
    cum_heads = jnp.transpose(cum_blocks, (0, 2, 1))
    log_gap = cum_heads[:, :, :, None] - cum_heads[:, :, None, :]
    decay = jnp.exp(jnp.where(lower_mask[None, None], log_gap, -1e30))
    step_heads = jnp.transpose(step_blocks, (0, 2, 1))
    weights = (intersection * decay * step_heads[:, :, None, :]).astype(jnp.bfloat16)
    local_part = jnp.einsum(
        "chtu,cuhp->cthp", weights, x_blocks, preferred_element_type=jnp.float32
    )
    last_cum = cum_blocks[:, SPAN - 1, :]
    x_weighted = (
        x_blocks.astype(jnp.float32)
        * (step_blocks * jnp.exp(last_cum[:, None, :] - cum_blocks))[:, :, :, None]
    ).astype(jnp.bfloat16)
    in_heads = jnp.repeat(in_map, per_group, axis=2)
    added = jnp.einsum("cuhp,cuhn->chpn", x_weighted, in_heads, preferred_element_type=jnp.float32)

    def carry_on(carried, element):
        block_decay, block_added = element
        return (block_decay[:, None, None] * carried + block_added, carried)

    empty_state = jnp.zeros((heads_here, HEAD_DIM, STATE), jnp.float32)
    device_state, entering = lax.scan(carry_on, empty_state, (jnp.exp(last_cum), added))
    device_decay = jnp.exp(jnp.sum(last_cum, axis=0))
    seeded = device_state + jnp.where(leading, device_decay[:, None, None] * init_state, 0.0)
    identity = (jnp.ones_like(device_decay), jnp.zeros_like(device_state))
    scanned = prefix_by_axis((device_decay, seeded), SEQ, combine, identity)
    incoming = jnp.where(leading, init_state, scanned[1])
    prefix = jnp.exp(jnp.cumsum(last_cum, axis=0) - last_cum)
    states_in = entering + prefix[:, :, None, None] * incoming[None]
    out_heads = jnp.repeat(out_map, per_group, axis=2).astype(jnp.float32)
    carried_part = (
        jnp.einsum("cthn,chpn->cthp", out_heads, states_in, precision=lax.Precision.HIGHEST)
        * jnp.exp(cum_blocks)[:, :, :, None]
    )
    ssm_out = local_part + carried_part + skip[None, None, :, None] * x_blocks.astype(jnp.float32)
    ssm_out = ssm_out.reshape(row_count, heads_here * HEAD_DIM)
    squares = taken_together(jnp.sum(ssm_out * ssm_out, axis=1), "tensor")
    mean_sq = squares / (HEADS * HEAD_DIM)
    normed = (ssm_out * lax.rsqrt(mean_sq + epsilon)[:, None] * norm_gain).astype(jnp.bfloat16)
    partial_out = jnp.dot(
        normed, lax.all_gather(w_out, SEQ, axis=1, tiled=True), preferred_element_type=jnp.float32
    )
    layer_out = sent_and_summed(partial_out.astype(jnp.bfloat16), "tensor", 0).astype(jnp.bfloat16)
    return (layer_out, abs_max)


def solution(mesh):
    finer = Mesh(mesh.devices.reshape(4, 8, mesh.shape["tensor"]), ("seq_0", "seq_1", "tensor"))
    return jax.shard_map(
        local,
        mesh=finer,
        in_specs=(
            P(SEQ_TENSOR, None),
            P(),
            P(SEQ, "tensor"),
            P(SEQ, "tensor", None, None),
            P(SEQ, "tensor"),
            P(None, "tensor"),
            P(None, "tensor", None, None),
            P(None, "tensor"),
            P(None, "tensor", None, None),
            P("tensor"),
            P("tensor"),
            P("tensor"),
            P("tensor", None, None),
            P("tensor"),
            P("tensor", SEQ),
        ),
        out_specs=(P(SEQ_TENSOR, None), P()),
        check_vma=False,
    )
```

profile of v0, /device:TPU:1, one launch (start us, length us, event | category | flops | bytes accessed | tf_op | source)
XLA Modules:
  0.0 373.7 jit_solution(1133156709951974368)
XLA Ops:
  7.2 0.9 copy.100
  8.1 0.8 copy.69
  8.9 1.7 pad_maximum_fusion.1
  10.6 2.6 broadcast_in_dim.26
  13.2 6.8 %all-to-all-start = ((bf16[8,32,4096]{2,1,0:T(8,128)(2,1)}), bf16[8,32,4096]{2,1,0:T(8,128)(2,1)S(1)}, u32[]{:S(2)}, u32[]{:S(2)}) async-start(bf16[8,32,4096]{2,1,0:T(8,128)(2,1)} %broadcast_in_dim.26), calls=%async_computation | async-start | bytes 4194304 | tf_op jit(solution)/shard_map/all_to_all | solution.py:27
  20.8 25.5 %all-to-all-done = bf16[8,32,4096]{2,1,0:T(8,128)(2,1)S(1)} async-done(((bf16[8,32,4096]{2,1,0:T(8,128)(2,1)}), bf16[8,32,4096]{2,1,0:T(8,128)(2,1)S(1)}, u32[]{:S(2)}, u32[]{:S(2)}) %all-to-all-start) | async-done | bytes 2097184 | tf_op jit(solution)/shard_map/all_to_all | solution.py:27
  46.3 2.6 fusion.5
  48.9 78.4 %all-gather.8.cloned.1.call-done = bf16[4096,1296]{1,0:T(8,128)(2,1)} async-done(((bf16[128,1296]{1,0:T(8,128)(2,1)}), bf16[4096,1296]{1,0:T(8,128)(2,1)}) %all-gather.8.cloned.1.call-update) | async-done | bytes 10616848 | tf_op jit(solution)/shard_map/all_gather | solution.py:47
  127.3 2.7 compare_select_fusion
  130.4 0.7 fusion.95
  131.1 2.3 fusion.20
  133.4 0.6 copy-done.5
  134.1 1.5 collective-permute-start.1
  135.6 5.7 %fusion.14 = bf16[256,1024]{1,0:T(8,128)(2,1)S(1)} fusion(bf16[256,4096]{1,0:T(8,128)(2,1)S(1)} %bitcast.201, bf16[4096,1296]{1,0:T(8,128)(2,1)} %all-gather.8.cloned.1.call-done, f32[]{:T(128)S(6)} %div.21), kind=kOutput, calls=%fused_computation.23 | convolution fusion | flops 2148007936 | bytes 11010052 | tf_op jit(solution)/shard_map/dot_general | solution.py:140
  141.3 3.2 collective-permute-start
  144.5 0.6 subtract_exponential_fusion
  145.1 1.0 copy.80
  146.1 1.3 multiply_convert_fusion.3
  147.5 0.8 fusion.96
  148.4 0.7 multiply_convert_fusion.2
  149.1 0.7 reshape.405
  149.8 0.9 copy.77
  151.0 2.0 while.13
  151.1 0.8 bitcast_dynamic-update-slice_fusion.2
  152.1 0.8 bitcast_dynamic-update-slice_fusion.2
  153.0 0.8 add_convert_fusion
  155.4 13.2 %all-reduce = bf16[128]{0:T(256)(128)(2,1)S(1)} all-reduce(bf16[128]{0:T(256)(128)(2,1)S(1)} %dynamic-update-slice), channel_id=2, replica_groups=mesh['seq_0'=4,'seq_1'=8,'tensor'=8] {'seq_1'}, use_global_device_ids=true, to_apply=%add | all-reduce | flops 128 | bytes 512
  168.6 0.7 broadcast_select_fusion.8
  169.3 20.5 %all-gather.14.cloned.1.call-done = bf16[128,64,128]{2,1,0:T(8,128)(2,1)} async-done(((bf16[16,64,128]{2,1,0:T(8,128)(2,1)}), bf16[128,64,128]{2,1,0:T(8,128)(2,1)}) %all-gather.14.cloned.1.call-update) | async-done | bytes 2097168 | tf_op jit(solution)/shard_map/all_gather | solution.py:68
  189.8 2.8 fusion.80
  193.3 8.1 %all-gather.2 = bf16[4,1,16]{2,1,0:T(2,128)(2,1)S(1)} all-gather(bf16[1,1,16]{2,1,0:T(2,128)(2,1)S(1)} %fusion.91), channel_id=1, replica_groups=mesh['seq_0'=4,'seq_1'=8,'tensor'=8] {'seq_0'}, dimensions={0}, use_global_device_ids=true | all-gather | bytes 160 | tf_op jit(solution)/shard_map/all_gather | solution.py:68
  201.6 1.1 copy.102
  202.8 1.9 convolution_bitcast_fusion.1
  204.8 15.7 %all-gather.10.cloned.1.call-done = bf16[4,16,64,128]{3,2,1,0:T(8,128)(2,1)} async-done(((bf16[1,16,64,128]{3,2,1,0:T(8,128)(2,1)}), bf16[4,16,64,128]{3,2,1,0:T(8,128)(2,1)}) %all-gather.10.cloned.1.call-update) | async-done | bytes 1048592 | tf_op jit(solution)/shard_map/all_gather | solution.py:68
  220.5 3.1 fusion.46
  223.7 2.2 multiply_reduce_fusion
  225.9 0.6 broadcast_in_dim.33
  226.5 7.1 %all-to-all-start.1 = ((f32[8,1,256]{2,1,0:T(1,128)}), f32[8,1,256]{2,1,0:T(1,128)S(1)}, u32[]{:S(2)}, u32[]{:S(2)}) async-start(f32[8,1,256]{2,1,0:T(1,128)} %broadcast_in_dim.33), calls=%async_computation.1 | async-start | bytes 16384 | tf_op jit(solution)/shard_map/all_to_all | solution.py:27
  233.5 0.8 copy.82
  234.4 3.8 %all-to-all-done.1 = f32[8,1,256]{2,1,0:T(1,128)S(1)} async-done(((f32[8,1,256]{2,1,0:T(1,128)}), f32[8,1,256]{2,1,0:T(1,128)S(1)}, u32[]{:S(2)}, u32[]{:S(2)}) %all-to-all-start.1) | async-done | bytes 8224 | tf_op jit(solution)/shard_map/all_to_all | solution.py:27
  238.2 1.3 broadcast_in_dim.35
  239.4 8.6 %all-to-all-start.3 = ((f32[32,1,1]{2,1,0:T(1,128)}), f32[32,1,1]{2,1,0:T(1,128)S(1)}, u32[]{:S(2)}, u32[]{:S(2)}) async-start(f32[32,1,1]{2,1,0:T(1,128)} %broadcast_in_dim.35), calls=%async_computation.3 | async-start | bytes 32768 | tf_op jit(solution)/shard_map/all_to_all | solution.py:27
  248.1 76.4 %all-gather.12.cloned.1.call-done = bf16[1024,4096]{1,0:T(8,128)(2,1)} async-done(((bf16[1024,128]{1,0:T(8,128)(2,1)}), bf16[1024,4096]{1,0:T(8,128)(2,1)}) %all-gather.12.cloned.1.call-update) | async-done | bytes 8388624 | tf_op jit(solution)/shard_map/all_gather | solution.py:210
  324.5 7.2 %convolution_convert_fusion = bf16[256,4096]{1,0:T(8,128)(2,1)} fusion(bf16[1024,4096]{1,0:T(8,128)(2,1)} %all-gather.12.cloned.1.call-done, f32[128,8,2,128]{3,2,1,0:T(2,128)S(1)} %bitcast.202, f32[1024]{0:T(1024)S(1)} %copy-done.6, f32[256]{0:T(256)S(1)} %add_rsqrt_fusion), kind=kOutput, calls=%fused_computation.8 | convolution fusion | flops 2149318656 | bytes 11539456 | tf_op jit(solution)/shard_map/dot_general | solution.py:209
  331.8 8.1 %all-to-all-start.2 = ((bf16[8,32,4096]{2,1,0:T(8,128)(2,1)}), bf16[8,32,4096]{2,1,0:T(8,128)(2,1)S(1)}, u32[]{:S(2)}, u32[]{:S(2)}) async-start(bf16[8,32,4096]{2,1,0:T(8,128)(2,1)} %bitcast.37), calls=%async_computation.2 | async-start | bytes 4194304 | tf_op jit(solution)/shard_map/all_to_all | solution.py:94
  339.9 0.6 reduce_max.19
  340.6 25.6 %all-to-all-done.2 = bf16[8,32,4096]{2,1,0:T(8,128)(2,1)S(1)} async-done(((bf16[8,32,4096]{2,1,0:T(8,128)(2,1)}), bf16[8,32,4096]{2,1,0:T(8,128)(2,1)S(1)}, u32[]{:S(2)}, u32[]{:S(2)}) %all-to-all-start.2) | async-done | bytes 2097184 | tf_op jit(solution)/shard_map/all_to_all | solution.py:94
  366.1 1.1 reduce_sum.42
  (84 shorter events, 3.3 us)
Async XLA Ops:
  7.2 120.2 %all-gather.8.cloned.1.call-start = ((), (), s32[]{:S(2)}) async-start(), calls=%async_computation.4 | async-start | bytes 11894784 | tf_op jit(solution)/shard_map/all_gather | solution.py:47
  13.2 7.5 %copy-start.11 = (f32[4,1,2,128]{3,2,1,0:T(2,128)S(1)}, f32[4,1,2,128]{3,2,1,0:T(2,128)}, u32[]{:S(2)}) copy-start(f32[4,1,2,128]{3,2,1,0:T(2,128)} %param.23) | copy-start | bytes 12292
  13.2 7.6 %copy-start.7 = (f32[4,1024]{1,0:T(4,128)S(1)}, f32[4,1024]{1,0:T(4,128)}, u32[]{:S(2)}) copy-start(f32[4,1024]{1,0:T(4,128)} %param.22) | copy-start | bytes 49156
  13.2 33.1 %all-to-all-start = ((bf16[8,32,4096]{2,1,0:T(8,128)(2,1)}), bf16[8,32,4096]{2,1,0:T(8,128)(2,1)S(1)}, u32[]{:S(2)}, u32[]{:S(2)}) async-start(bf16[8,32,4096]{2,1,0:T(8,128)(2,1)} %broadcast_in_dim.26), calls=%async_computation | async-start | bytes 4194304 | tf_op jit(solution)/shard_map/all_to_all | solution.py:27
  20.1 169.8 %all-gather.14.cloned.1.call-start = ((), (), s32[]{:S(2)}) async-start(), calls=%async_computation.7 | async-start | bytes 2359296 | tf_op jit(solution)/shard_map/all_gather | solution.py:68
  20.8 106.5 %copy-start.15 = (f32[16]{0:T(128)S(1)}, f32[16]{0:T(128)}, u32[]{:S(2)}) copy-start(f32[16]{0:T(128)} %param.26) | copy-start | bytes 196
  48.9 81.2 %copy-start.16 = (f32[16]{0:T(128)S(1)}, f32[16]{0:T(128)}, u32[]{:S(2)}) copy-start(f32[16]{0:T(128)} %param.27) | copy-start | bytes 196
  127.3 3.8 %copy-start = (bf16[8,32,4096]{2,1,0:T(8,128)(2,1)S(1)}, bf16[8,32,4096]{2,1,0:T(8,128)(2,1)}, u32[]{:S(2)}) copy-start(bf16[8,32,4096]{2,1,0:T(8,128)(2,1)} %get-tuple-element.61) | copy-start | bytes 6291460
  133.4 0.7 copy-start.5
  134.1 12.1 %copy-start.14 = (bf16[3,1,2,128]{3,2,1,0:T(2,128)(2,1)S(1)}, bf16[3,1,2,128]{3,2,1,0:T(2,128)(2,1)}, u32[]{:S(2)}) copy-start(bf16[3,1,2,128]{3,2,1,0:T(2,128)(2,1)} %param.25) | copy-start | bytes 4612
  134.1 14.3 %copy-start.8 = (bf16[3,1024]{1,0:T(4,128)(2,1)S(1)}, bf16[3,1024]{1,0:T(4,128)(2,1)}, u32[]{:S(2)}) copy-start(bf16[3,1024]{1,0:T(4,128)(2,1)} %param.24) | copy-start | bytes 18436
  134.1 12.0 %collective-permute-start.1 = (bf16[3,256]{1,0:T(4,128)(2,1)S(1)}, bf16[3,256]{1,0:T(4,128)(2,1)S(1)}, u32[]{:S(2)}, u32[]{:S(2)}) collective-permute-start(bf16[3,256]{1,0:T(4,128)(2,1)S(1)} %slice.201), channel_id=1, source_target_pairs={{0,8},{8,16},{16,24},{24,32},{32,40},{40,48},{48,56},{56,64},{64,7... | collective-permute-start | bytes 4616 | tf_op jit(solution)/shard_map/ppermute | solution.py:53
  141.3 7.0 %collective-permute-start = (bf16[3,1024]{1,0:T(4,128)(2,1)S(1)}, bf16[3,1024]{1,0:T(4,128)(2,1)S(1)}, u32[]{:S(2)}, u32[]{:S(2)}) collective-permute-start(bf16[3,1024]{1,0:T(4,128)(2,1)S(1)} %slice.196), channel_id=1, source_target_pairs={{0,8},{8,16},{16,24},{24,32},{32,40},{40,48},{48,56},{56,64},{64,7... | collective-permute-start | bytes 18440 | tf_op jit(solution)/shard_map/ppermute | solution.py:53
  151.0 2.0 copy-start.2
  151.0 3.0 copy-start.18
  153.9 66.6 %all-gather.10.cloned.1.call-start = ((), (), s32[]{:S(2)}) async-start(), calls=%async_computation.5 | async-start | bytes 1310720 | tf_op jit(solution)/shard_map/all_gather | solution.py:68
  169.2 32.2 %copy-start.9 = (f32[16]{0:T(128)}, f32[16]{0:T(128)S(1)}, u32[]{:S(2)}) copy-start(f32[16]{0:T(128)S(1)} %get-tuple-element.82) | copy-start | bytes 196
  192.6 131.9 %all-gather.12.cloned.1.call-start = ((), (), s32[]{:S(2)}) async-start(), calls=%async_computation.6 | async-start | bytes 8650752 | tf_op jit(solution)/shard_map/all_gather | solution.py:210
  201.6 18.9 %copy-start.1 = (bf16[128,64,128]{2,1,0:T(8,128)(2,1)S(1)}, bf16[128,64,128]{2,1,0:T(8,128)(2,1)}, u32[]{:S(2)}) copy-start(bf16[128,64,128]{2,1,0:T(8,128)(2,1)} %all-gather.14.cloned.1.call-done) | copy-start | bytes 6291460
  201.6 18.9 %copy-start.10 = (f32[16]{0:T(128)S(1)}, f32[16]{0:T(128)}, u32[]{:S(2)}) copy-start(f32[16]{0:T(128)} %copy-done.9) | copy-start | bytes 196
  201.6 18.9 %copy-start.13 = (f32[16]{0:T(128)S(1)}, f32[16]{0:T(128)}, u32[]{:S(2)}) copy-start(f32[16]{0:T(128)} %get-tuple-element.81) | copy-start | bytes 196
  220.5 3.2 copy-start.3
  220.5 3.2 copy-start.4
  220.5 3.2 copy-start.12
  220.5 3.2 copy-start.17
  225.9 98.6 %copy-start.6 = (f32[1024]{0:T(1024)S(1)}, f32[1024]{0:T(1024)}, u32[]{:S(2)}) copy-start(f32[1024]{0:T(1024)} %param.30) | copy-start | bytes 12292
  226.5 11.7 %all-to-all-start.1 = ((f32[8,1,256]{2,1,0:T(1,128)}), f32[8,1,256]{2,1,0:T(1,128)S(1)}, u32[]{:S(2)}, u32[]{:S(2)}) async-start(f32[8,1,256]{2,1,0:T(1,128)} %broadcast_in_dim.33), calls=%async_computation.1 | async-start | bytes 16384 | tf_op jit(solution)/shard_map/all_to_all | solution.py:27
  239.4 92.3 %all-to-all-start.3 = ((f32[32,1,1]{2,1,0:T(1,128)}), f32[32,1,1]{2,1,0:T(1,128)S(1)}, u32[]{:S(2)}, u32[]{:S(2)}) async-start(f32[32,1,1]{2,1,0:T(1,128)} %broadcast_in_dim.35), calls=%async_computation.3 | async-start | bytes 32768 | tf_op jit(solution)/shard_map/all_to_all | solution.py:27
  331.8 34.4 %all-to-all-start.2 = ((bf16[8,32,4096]{2,1,0:T(8,128)(2,1)}), bf16[8,32,4096]{2,1,0:T(8,128)(2,1)S(1)}, u32[]{:S(2)}, u32[]{:S(2)}) async-start(bf16[8,32,4096]{2,1,0:T(8,128)(2,1)} %bitcast.37), calls=%async_computation.2 | async-start | bytes 4194304 | tf_op jit(solution)/shard_map/all_to_all | solution.py:94
Sparse Core Ops, SparseCore 0:
  10.7 116.5 all-gather.7
  154.0 35.7 all-gather.13
  192.8 27.6 all-gather.9
  222.8 101.6 all-gather.11
where the time goes:
time: 375 us; the launch traced here: 374 us
  waiting for transfers between devices  247 us (66%)
  starting transfers between devices  35.5 us (9%)
  matrix products  22.6 us (6%)
  blocking collectives  21.3 us (6%)
  other arithmetic  19.1 us (5%)
  between operations  15.4 us (4%)
  local copies, waits for them, and re-layouts  13.2 us (4%)
    all_gather x1, waiting for transfers between devices, sent_together(): lax.all_gather(both, axis, axis=dim, tiled=True)  78.4 us
    all_gather x1, waiting for transfers between devices, local(): lax.all_gather(w_out, SEQ, axis=1, tiled=True)  76.4 us
    all_gather x2, waiting for transfers between devices, prefix_by_axis(): lax.all_gather(part.astype(kind), axis)  36.2 us
    all_to_all x3, waiting for transfers between devices, sent_to_all(): lax.all_to_all(jnp.broadcast_to(shard[None], (count, *shard.shape)), axis...  29.3 us
    all_to_all x1, waiting for transfers between devices, sent_and_summed(): lax.all_to_all(parts, axis, split_axis=0, concat_axis=0, tiled=True)  25.6 us
    all_to_all x3, starting transfers between devices, sent_to_all(): lax.all_to_all(jnp.broadcast_to(shard[None], (count, *shard.shape)), axis...  22.5 us
    unnamed x1, blocking collectives  13.2 us
    dot_general x3, matrix products, local(): jnp.dot(quant, weight_piece, preferred_element_type=jnp.float32)  10.7 us
  transfers between devices with their start and end apart: 10, of which 7 were waited for; matrix products, arithmetic and copies ran while one was open for 10% of the time, Pallas kernels for 0%

commit v1 on v0

--- a/solution.py
+++ b/solution.py
@@ -206,9 +206,13 @@
     squares = taken_together(jnp.sum(ssm_out * ssm_out, axis=1), "tensor")
     mean_sq = squares / (HEADS * HEAD_DIM)
     normed = (ssm_out * lax.rsqrt(mean_sq + epsilon)[:, None] * norm_gain).astype(jnp.bfloat16)
-    partial_out = jnp.dot(
-        normed, lax.all_gather(w_out, SEQ, axis=1, tiled=True), preferred_element_type=jnp.float32
-    )
+    obtain_leaf = lambda v0, join_dim: jnp.concatenate(
+        lax.all_to_all(
+            jnp.stack(lax.axis_size(SEQ) * [v0]), axis_name=SEQ, split_axis=0, concat_axis=0
+        ),
+        join_dim,
+    )
+    partial_out = jnp.dot(normed, obtain_leaf(w_out, 1), preferred_element_type=jnp.float32)
     layer_out = sent_and_summed(partial_out.astype(jnp.bfloat16), "tensor", 0).astype(jnp.bfloat16)
     return (layer_out, abs_max)
 

time: 375 us -> 501 us (1.34)
  waiting for transfers between devices: 247 us -> 362 us
  starting transfers between devices: 35.5 us -> 42.8 us
    all_to_all x0 -> x1, waiting for transfers between devices: none -> 187 us  [local(): lax.all_to_all(jnp.stack(lax.axis_size(SEQ) * [v0]), axis_name=SEQ, split...]
    all_gather x1 -> x0, waiting for transfers between devices: 76.4 us -> none  [local(): lax.all_gather(w_out, SEQ, axis=1, tiled=True)]
    all_to_all x0 -> x1, starting transfers between devices: none -> 8.9 us  [local(): lax.all_to_all(jnp.stack(lax.axis_size(SEQ) * [v0]), axis_name=SEQ, split...]
  transfers between devices with their start and end apart: 10 -> 10, of which waited for: 7 -> 9; matrix products, arithmetic and copies ran while one was open for 10% -> 5% of each run, Pallas kernels for 0% -> 0%
where the time goes in v1:
time: 501 us; the launch traced here: 500 us
  waiting for transfers between devices  362 us (72%)
  starting transfers between devices  42.8 us (9%)
  matrix products  22.5 us (4%)
  blocking collectives  22.1 us (4%)
  other arithmetic  19.4 us (4%)
  local copies, waits for them, and re-layouts  15.9 us (3%)
  between operations  15.5 us (3%)
    all_to_all x1, waiting for transfers between devices, local(): lax.all_to_all(jnp.stack(lax.axis_size(SEQ) * [v0]), axis_name=SEQ, split...  187 us
    all_gather x1, waiting for transfers between devices, sent_together(): lax.all_gather(both, axis, axis=dim, tiled=True)  78.4 us
    all_gather x2, waiting for transfers between devices, prefix_by_axis(): lax.all_gather(part.astype(kind), axis)  38.9 us
    all_to_all x3, waiting for transfers between devices, sent_to_all(): lax.all_to_all(jnp.broadcast_to(shard[None], (count, *shard.shape)), axis...  31.4 us
    all_to_all x1, waiting for transfers between devices, sent_and_summed(): lax.all_to_all(parts, axis, split_axis=0, concat_axis=0, tiled=True)  25.6 us
    all_to_all x3, starting transfers between devices, sent_to_all(): lax.all_to_all(jnp.broadcast_to(shard[None], (count, *shard.shape)), axis...  23.4 us
    unnamed x1, blocking collectives  14 us
    dot_general x3, matrix products, local(): jnp.dot(quant, weight_piece, preferred_element_type=jnp.float32)  10.7 us
  transfers between devices with their start and end apart: 10, of which 9 were waited for; matrix products, arithmetic and copies ran while one was open for 5% of the time, Pallas kernels for 0%

profile of v1, /device:TPU:1, one launch (start us, length us, event | category | flops | bytes accessed | tf_op | source)
XLA Modules:
  0.0 500.1 jit_solution(11263866153296743387)
XLA Ops:
  7.2 0.9 copy.106
  8.1 0.8 copy.72
  8.9 1.7 pad_maximum_fusion.1
  10.6 2.6 broadcast_in_dim.26
  13.2 6.8 %all-to-all-start = ((bf16[8,32,4096]{2,1,0:T(8,128)(2,1)}), bf16[8,32,4096]{2,1,0:T(8,128)(2,1)S(1)}, u32[]{:S(2)}, u32[]{:S(2)}) async-start(bf16[8,32,4096]{2,1,0:T(8,128)(2,1)} %broadcast_in_dim.26), calls=%async_computation | async-start | bytes 4194304 | tf_op jit(solution)/shard_map/all_to_all | solution.py:27
  20.8 25.5 %all-to-all-done = bf16[8,32,4096]{2,1,0:T(8,128)(2,1)S(1)} async-done(((bf16[8,32,4096]{2,1,0:T(8,128)(2,1)}), bf16[8,32,4096]{2,1,0:T(8,128)(2,1)S(1)}, u32[]{:S(2)}, u32[]{:S(2)}) %all-to-all-start) | async-done | bytes 2097184 | tf_op jit(solution)/shard_map/all_to_all | solution.py:27
  46.3 2.6 fusion.5
  48.9 78.4 %all-gather.7.cloned.1.call-done = bf16[4096,1296]{1,0:T(8,128)(2,1)} async-done(((bf16[128,1296]{1,0:T(8,128)(2,1)}), bf16[4096,1296]{1,0:T(8,128)(2,1)}) %all-gather.7.cloned.1.call-update) | async-done | bytes 10616848 | tf_op jit(solution)/shard_map/all_gather | solution.py:47
  127.3 2.7 compare_select_fusion
  130.5 5.7 %fusion.14 = bf16[256,1024]{1,0:T(8,128)(2,1)S(1)} fusion(bf16[256,4096]{1,0:T(8,128)(2,1)S(1)} %bitcast.201, bf16[4096,1296]{1,0:T(8,128)(2,1)} %all-gather.7.cloned.1.call-done, f32[]{:T(128)S(6)} %div.21), kind=kOutput, calls=%fused_computation.23 | convolution fusion | flops 2148007936 | bytes 11010052 | tf_op jit(solution)/shard_map/dot_general | solution.py:140
  136.2 1.6 collective-permute-start
  137.8 2.3 fusion.20
  140.1 3.2 collective-permute-start.1
  143.3 0.6 subtract_exponential_fusion
  144.3 0.8 fusion.93
  145.1 2.6 multiply_convert_fusion.3
  147.8 0.7 reshape.429
  148.4 0.9 copy.80
  149.7 2.0 while.13
  149.7 0.8 bitcast_dynamic-update-slice_fusion.2
  150.7 0.8 bitcast_dynamic-update-slice_fusion.2
  151.7 0.8 add_convert_fusion
  152.7 0.6 dynamic-slice
  154.1 14.0 %all-reduce = bf16[128]{0:T(256)(128)(2,1)S(1)} all-reduce(bf16[128]{0:T(256)(128)(2,1)S(1)} %dynamic-update-slice), channel_id=2, replica_groups=mesh['seq_0'=4,'seq_1'=8,'tensor'=8] {'seq_1'}, use_global_device_ids=true, to_apply=%add | all-reduce | flops 128 | bytes 512
  168.2 0.6 broadcast_select_fusion.8
  168.9 22.7 %all-gather.11.cloned.1.call-done = bf16[128,64,128]{2,1,0:T(8,128)(2,1)} async-done(((bf16[16,64,128]{2,1,0:T(8,128)(2,1)}), bf16[128,64,128]{2,1,0:T(8,128)(2,1)}) %all-gather.11.cloned.1.call-update) | async-done | bytes 2097168 | tf_op jit(solution)/shard_map/all_gather | solution.py:68
  191.6 2.8 fusion.77
  194.5 8.1 %all-gather.2 = bf16[4,1,16]{2,1,0:T(2,128)(2,1)S(1)} all-gather(bf16[1,1,16]{2,1,0:T(2,128)(2,1)S(1)} %fusion.88), channel_id=1, replica_groups=mesh['seq_0'=4,'seq_1'=8,'tensor'=8] {'seq_0'}, dimensions={0}, use_global_device_ids=true | all-gather | bytes 160 | tf_op jit(solution)/shard_map/all_gather | solution.py:68
  202.7 1.1 copy.108
  204.0 1.9 convolution_bitcast_fusion.1
  205.9 16.1 %all-gather.9.cloned.1.call-done = bf16[4,16,64,128]{3,2,1,0:T(8,128)(2,1)} async-done(((bf16[1,16,64,128]{3,2,1,0:T(8,128)(2,1)}), bf16[4,16,64,128]{3,2,1,0:T(8,128)(2,1)}) %all-gather.9.cloned.1.call-update) | async-done | bytes 1048592 | tf_op jit(solution)/shard_map/all_gather | solution.py:68
  222.1 3.1 fusion.44
  225.2 2.2 multiply_reduce_fusion
  227.4 0.6 broadcast_in_dim.33
  228.0 7.0 %all-to-all-start.1 = ((f32[8,1,256]{2,1,0:T(1,128)}), f32[8,1,256]{2,1,0:T(1,128)S(1)}, u32[]{:S(2)}, u32[]{:S(2)}) async-start(f32[8,1,256]{2,1,0:T(1,128)} %broadcast_in_dim.33), calls=%async_computation.1 | async-start | bytes 16384 | tf_op jit(solution)/shard_map/all_to_all | solution.py:27
  235.2 4.5 all-to-all-done.1
  239.7 4.3 stack.2
  244.0 8.9 %all-to-all-start.2 = ((bf16[32,1024,128]{1,2,0:T(8,128)(2,1)}), bf16[32,1024,128]{1,2,0:T(8,128)(2,1)}, u32[]{:S(2)}, u32[]{:S(2)}) async-start(bf16[32,1024,128]{1,2,0:T(8,128)(2,1)} %stack.2), calls=%async_computation.2 | async-start | bytes 16777216 | tf_op jit(solution)/shard_map/all_to_all | solution.py:210
  253.3 0.5 copy.86
  253.8 187.4 %all-to-all-done.2 = bf16[32,1024,128]{1,2,0:T(8,128)(2,1)} async-done(((bf16[32,1024,128]{1,2,0:T(8,128)(2,1)}), bf16[32,1024,128]{1,2,0:T(8,128)(2,1)}, u32[]{:S(2)}, u32[]{:S(2)}) %all-to-all-start.2) | async-done | bytes 8388640 | tf_op jit(solution)/shard_map/all_to_all | solution.py:210
  441.2 1.3 broadcast_in_dim.35
  442.4 9.6 %all-to-all-start.4 = ((f32[32,1,1]{2,1,0:T(1,128)}), f32[32,1,1]{2,1,0:T(1,128)S(1)}, u32[]{:S(2)}, u32[]{:S(2)}) async-start(f32[32,1,1]{2,1,0:T(1,128)} %broadcast_in_dim.35), calls=%async_computation.4 | async-start | bytes 32768 | tf_op jit(solution)/shard_map/all_to_all | solution.py:27
  452.0 7.2 %convolution_convert_fusion = bf16[256,4096]{1,0:T(8,128)(2,1)} fusion(bf16[1024,4096]{0,1:T(8,128)(2,1)} %bitcast.39, bf16[128,8,2,128]{3,2,1,0:T(2,128)(2,1)S(1)} %bitcast.209), kind=kOutput, calls=%fused_computation.8 | convolution fusion | flops 2148532224 | bytes 11010048 | tf_op jit(solution)/shard_map/dot_general | solution.py:215
  459.1 1.4 all-to-all-done.4
  460.6 5.7 %all-to-all-start.3 = ((bf16[8,32,4096]{2,1,0:T(8,128)(2,1)}), bf16[8,32,4096]{2,1,0:T(8,128)(2,1)S(1)}, u32[]{:S(2)}, u32[]{:S(2)}) async-start(bf16[8,32,4096]{2,1,0:T(8,128)(2,1)} %bitcast.203), calls=%async_computation.3 | async-start | bytes 4194304 | tf_op jit(solution)/shard_map/all_to_all | solution.py:94
  466.2 0.6 reduce_max.19
  466.9 25.6 %all-to-all-done.3 = bf16[8,32,4096]{2,1,0:T(8,128)(2,1)S(1)} async-done(((bf16[8,32,4096]{2,1,0:T(8,128)(2,1)}), bf16[8,32,4096]{2,1,0:T(8,128)(2,1)S(1)}, u32[]{:S(2)}, u32[]{:S(2)}) %all-to-all-start.3) | async-done | bytes 2097184 | tf_op jit(solution)/shard_map/all_to_all | solution.py:94
  492.5 1.1 reduce_sum.42
  (89 shorter events, 3.0 us)
Async XLA Ops:
  7.2 120.2 %all-gather.7.cloned.1.call-start = ((), (), s32[]{:S(2)}) async-start(), calls=%async_computation.5 | async-start | bytes 11894784 | tf_op jit(solution)/shard_map/all_gather | solution.py:47
  13.2 7.5 %copy-start.12 = (f32[4,1,2,128]{3,2,1,0:T(2,128)S(1)}, f32[4,1,2,128]{3,2,1,0:T(2,128)}, u32[]{:S(2)}) copy-start(f32[4,1,2,128]{3,2,1,0:T(2,128)} %param.23) | copy-start | bytes 12292
  13.2 7.6 %copy-start.7 = (f32[4,1024]{1,0:T(4,128)S(1)}, f32[4,1024]{1,0:T(4,128)}, u32[]{:S(2)}) copy-start(f32[4,1024]{1,0:T(4,128)} %param.22) | copy-start | bytes 49156
  13.2 33.1 %all-to-all-start = ((bf16[8,32,4096]{2,1,0:T(8,128)(2,1)}), bf16[8,32,4096]{2,1,0:T(8,128)(2,1)S(1)}, u32[]{:S(2)}, u32[]{:S(2)}) async-start(bf16[8,32,4096]{2,1,0:T(8,128)(2,1)} %broadcast_in_dim.26), calls=%async_computation | async-start | bytes 4194304 | tf_op jit(solution)/shard_map/all_to_all | solution.py:27
  20.1 171.5 %all-gather.11.cloned.1.call-start = ((), (), s32[]{:S(2)}) async-start(), calls=%async_computation.7 | async-start | bytes 2359296 | tf_op jit(solution)/shard_map/all_gather | solution.py:68
  20.8 106.5 %copy-start.16 = (f32[16]{0:T(128)S(1)}, f32[16]{0:T(128)}, u32[]{:S(2)}) copy-start(f32[16]{0:T(128)} %param.26) | copy-start | bytes 196
  48.9 81.2 %copy-start.17 = (f32[16]{0:T(128)S(1)}, f32[16]{0:T(128)}, u32[]{:S(2)}) copy-start(f32[16]{0:T(128)} %param.27) | copy-start | bytes 196
  127.3 3.1 copy-start
  136.2 3.9 copy-start.5
  136.2 7.8 %copy-start.15 = (bf16[3,1,2,128]{3,2,1,0:T(2,128)(2,1)S(1)}, bf16[3,1,2,128]{3,2,1,0:T(2,128)(2,1)}, u32[]{:S(2)}) copy-start(bf16[3,1,2,128]{3,2,1,0:T(2,128)(2,1)} %param.25) | copy-start | bytes 4612
  136.2 8.9 %copy-start.8 = (bf16[3,1024]{1,0:T(4,128)(2,1)S(1)}, bf16[3,1024]{1,0:T(4,128)(2,1)}, u32[]{:S(2)}) copy-start(bf16[3,1024]{1,0:T(4,128)(2,1)} %param.24) | copy-start | bytes 18436
  136.2 8.9 %collective-permute-start = (bf16[3,1024]{1,0:T(4,128)(2,1)S(1)}, bf16[3,1024]{1,0:T(4,128)(2,1)S(1)}, u32[]{:S(2)}, u32[]{:S(2)}) collective-permute-start(bf16[3,1024]{1,0:T(4,128)(2,1)S(1)} %slice.196), channel_id=1, source_target_pairs={{0,8},{8,16},{16,24},{24,32},{32,40},{40,48},{48,56},{56,64},{64,7... | collective-permute-start | bytes 18440 | tf_op jit(solution)/shard_map/ppermute | solution.py:53
  140.1 3.9 collective-permute-start.1
  149.7 2.0 copy-start.2
  149.7 3.0 copy-start.19
  152.6 69.5 %all-gather.9.cloned.1.call-start = ((), (), s32[]{:S(2)}) async-start(), calls=%async_computation.6 | async-start | bytes 1310720 | tf_op jit(solution)/shard_map/all_gather | solution.py:68
  168.8 33.8 %copy-start.9 = (f32[16]{0:T(128)}, f32[16]{0:T(128)S(1)}, u32[]{:S(2)}) copy-start(f32[16]{0:T(128)S(1)} %get-tuple-element.82) | copy-start | bytes 196
  202.7 19.3 %copy-start.1 = (bf16[128,64,128]{2,1,0:T(8,128)(2,1)S(1)}, bf16[128,64,128]{2,1,0:T(8,128)(2,1)}, u32[]{:S(2)}) copy-start(bf16[128,64,128]{2,1,0:T(8,128)(2,1)} %all-gather.11.cloned.1.call-done) | copy-start | bytes 6291460
  202.7 19.3 %copy-start.10 = (f32[16]{0:T(128)S(1)}, f32[16]{0:T(128)}, u32[]{:S(2)}) copy-start(f32[16]{0:T(128)} %copy-done.9) | copy-start | bytes 196
  202.7 19.3 %copy-start.14 = (f32[16]{0:T(128)S(1)}, f32[16]{0:T(128)}, u32[]{:S(2)}) copy-start(f32[16]{0:T(128)} %get-tuple-element.81) | copy-start | bytes 196
  222.0 3.2 copy-start.3
  222.0 3.2 copy-start.4
  222.0 3.2 copy-start.13
  222.1 3.2 copy-start.18
  225.2 9.9 %copy-start.6 = (bf16[1024,128]{1,0:T(8,128)(2,1)S(1)}, bf16[1024,128]{1,0:T(8,128)(2,1)}, u32[]{:S(2)}) copy-start(bf16[1024,128]{1,0:T(8,128)(2,1)} %param.31) | copy-start | bytes 786436
  228.0 11.7 %all-to-all-start.1 = ((f32[8,1,256]{2,1,0:T(1,128)}), f32[8,1,256]{2,1,0:T(1,128)S(1)}, u32[]{:S(2)}, u32[]{:S(2)}) async-start(f32[8,1,256]{2,1,0:T(1,128)} %broadcast_in_dim.33), calls=%async_computation.1 | async-start | bytes 16384 | tf_op jit(solution)/shard_map/all_to_all | solution.py:27
  244.0 8.9 %copy-start.11 = (f32[1024]{0:T(1024)S(1)}, f32[1024]{0:T(1024)}, u32[]{:S(2)}) copy-start(f32[1024]{0:T(1024)} %param.30) | copy-start | bytes 12292
  244.0 197.2 %all-to-all-start.2 = ((bf16[32,1024,128]{1,2,0:T(8,128)(2,1)}), bf16[32,1024,128]{1,2,0:T(8,128)(2,1)}, u32[]{:S(2)}, u32[]{:S(2)}) async-start(bf16[32,1024,128]{1,2,0:T(8,128)(2,1)} %stack.2), calls=%async_computation.2 | async-start | bytes 16777216 | tf_op jit(solution)/shard_map/all_to_all | solution.py:210
  442.4 18.2 %all-to-all-start.4 = ((f32[32,1,1]{2,1,0:T(1,128)}), f32[32,1,1]{2,1,0:T(1,128)S(1)}, u32[]{:S(2)}, u32[]{:S(2)}) async-start(f32[32,1,1]{2,1,0:T(1,128)} %broadcast_in_dim.35), calls=%async_computation.4 | async-start | bytes 32768 | tf_op jit(solution)/shard_map/all_to_all | solution.py:27
  460.6 31.9 %all-to-all-start.3 = ((bf16[8,32,4096]{2,1,0:T(8,128)(2,1)}), bf16[8,32,4096]{2,1,0:T(8,128)(2,1)S(1)}, u32[]{:S(2)}, u32[]{:S(2)}) async-start(bf16[8,32,4096]{2,1,0:T(8,128)(2,1)} %bitcast.203), calls=%async_computation.3 | async-start | bytes 4194304 | tf_op jit(solution)/shard_map/all_to_all | solution.py:94
Sparse Core Ops, SparseCore 0:
  10.7 116.5 all-gather.6
  152.7 38.8 all-gather.10
  194.5 27.4 all-gather.8
